TPU v7x, 256 devices: a whole 4x4x8 slice. The times are simulated.
256 devices in a mesh: gx: 32 (over z, x_hi, core), gy: 8 (over x_lo, y).
Axes of the slice: x: 4 (x_hi: 2, x_lo: 2; x = x_hi * 2 + x_lo), y: 4, z: 8, core: 2. Of those that a mesh axis runs over, the one named last changes fastest.
Arguments:
- features: bfloat16 [384, 512, 256], P('gy', 'gx'), may hold values from -6 to 6
- first_filter: bfloat16 [256, 3, 3, 256], P('gy'), may hold values from -0.125 to 0.125
- second_filter: bfloat16 [256, 3, 3, 256], P('gy'), may hold values from -0.125 to 0.125
- cotangent: bfloat16 [256, 512, 384], P('gy', 'gx'), may hold values from -6 to 6
Outputs:
- output: bfloat16 [256, 512, 384], P('gy', 'gx')
- input_grad: bfloat16 [384, 512, 256], P('gy', 'gx')
- first_grad: float32 [256, 3, 3, 256], P('gy')
- second_grad: float32 [256, 3, 3, 256], P('gy')
All inputs are finite; a program needn't handle non-finite values.
Results may differ from a plain program's by a relative error of at most 0.0059.
Values may be sent and summed in bfloat16 or wider, within the bound.
A program may use at most 128 MiB of HBM per device.

v0:
```python
import math

import jax
import jax.numpy as jnp
from jax import lax
from jax.sharding import PartitionSpec as P


def padded_2(block, sides, width):
    for axis, dim in sides:
        count = lax.axis_size(axis)
        forward = [(i, i + 1) for i in range(count - 1)]
        backward = [(target, source) for source, target in forward]
        low = lax.ppermute(
            lax.slice_in_dim(block, block.shape[dim] - width, None, axis=dim), axis, forward
        )
        high = lax.ppermute(lax.slice_in_dim(block, 0, width, axis=dim), axis, backward)
        block = jnp.concatenate([low, block, high], axis=dim)
    return block


def silu_parts(pre):
    sigma = jax.nn.sigmoid(pre)
    return (pre * sigma, sigma * (1.0 + pre * (1.0 - sigma)))


def conv_taps(padded, weight, height, width):
    total = jnp.zeros((height * width, weight.shape[3]), jnp.float32)
    for i in range(3):
        for j in range(3):
            window = padded[i : i + height, j : j + width, :].reshape(
                height * width, padded.shape[2]
            )
            total = total + jnp.dot(window, weight[i, j], preferred_element_type=jnp.float32)
    return total.reshape(height, width, weight.shape[3])


def flipped(weight):
    return jnp.transpose(weight[::-1, ::-1], (0, 1, 3, 2))


def filter_grad(padded, grad, height, width):
    flat_grad = grad.reshape(height * width, grad.shape[2])
    tap_list = []
    for i in range(3):
        for j in range(3):
            window = padded[i : i + height, j : j + width, :].reshape(
                height * width, padded.shape[2]
            )
            tap_list.append(
                lax.dot_general(
                    window, flat_grad, (((0,), (0,)), ((), ())), preferred_element_type=jnp.float32
                )
            )
    return jnp.stack(tap_list).reshape(3, 3, padded.shape[2], grad.shape[2])


def to_taps(weight):
    return jnp.transpose(weight, (1, 2, 3, 0))


def from_taps(weight):
    return jnp.transpose(weight, (3, 0, 1, 2))


def block_rim(field):
    return padded_2(field, (("gy", 0), ("gx", 1)), 1)


def body(features, first_filter, second_filter, cotangent):
    band_count = lax.axis_size("gy")
    strip_count = lax.axis_size("gx")
    block_rows = features.shape[0]
    strip_width = features.shape[1]
    scale_factor = 1.0 / math.sqrt(block_rows * band_count * strip_width * strip_count)
    first_whole, second_whole = (
        lax.all_gather(first_filter, "gy", axis=0, tiled=True),
        lax.all_gather(second_filter, "gy", axis=0, tiled=True),
    )
    first_taps = to_taps(first_whole)
    second_taps = to_taps(second_whole)
    feat_padded = block_rim(features)
    first_pre = conv_taps(feat_padded, first_taps, block_rows, strip_width)
    first_act, first_slope = silu_parts(first_pre)
    hidden = first_act.astype(jnp.bfloat16)
    hidden_padded = block_rim(hidden)
    second_pre = conv_taps(hidden_padded, second_taps, block_rows, strip_width)
    second_act, second_slope = silu_parts(second_pre)
    output_block = jnp.transpose(second_act.astype(jnp.bfloat16), (2, 1, 0))
    output = lax.all_to_all(output_block, "gy", split_axis=0, concat_axis=2, tiled=True)
    block_cot = lax.all_to_all(cotangent, "gy", split_axis=2, concat_axis=0, tiled=True)
    cot_map = jnp.transpose(block_cot, (2, 1, 0))
    outer_grad = (cot_map.astype(jnp.float32) * second_slope).astype(jnp.bfloat16)
    second_local = filter_grad(hidden_padded, outer_grad, block_rows, strip_width) * scale_factor
    hidden_grad = conv_taps(block_rim(outer_grad), flipped(second_taps), block_rows, strip_width)
    inner_grad = (hidden_grad * first_slope).astype(jnp.bfloat16)
    first_local = filter_grad(feat_padded, inner_grad, block_rows, strip_width) * scale_factor
    input_grad = conv_taps(
        block_rim(inner_grad), flipped(first_taps), block_rows, strip_width
    ).astype(jnp.bfloat16)
    first_part, second_part = (
        lax.psum_scatter(from_taps(first_local), "gy", scatter_dimension=0, tiled=True),
        lax.psum_scatter(from_taps(second_local), "gy", scatter_dimension=0, tiled=True),
    )
    first_grad, second_grad = lax.psum((first_part, second_part), "gx")
    return (output, input_grad, first_grad, second_grad)


def solution(mesh):
    in_specs = (
        P("gy", "gx", None),
        P("gy", None, None, None),
        P("gy", None, None, None),
        P("gy", "gx", None),
    )
    out_specs = (
        P("gy", "gx", None),
        P("gy", "gx", None),
        P("gy", None, None, None),
        P("gy", None, None, None),
    )
    return jax.shard_map(body, mesh=mesh, in_specs=in_specs, out_specs=out_specs, check_vma=False)
```

profile of v0, /device:TPU:1, one launch (start us, length us, event | category | flops | bytes accessed | tf_op | source)
XLA Modules:
  0.0 497.4 jit_solution(1822086742639933650)
XLA Ops:
  7.9 1.1 copy.181
  9.1 1.3 collective-permute-start.1
  10.4 4.6 collective-permute-start
  15.0 1.3 copy.209
  16.4 2.2 reshape.212
  18.6 6.3 %all-to-all-start.1 = ((bf16[8,2,12288]{2,1,0:T(2,128)(2,1)}), bf16[8,2,12288]{2,1,0:T(2,128)(2,1)S(1)}, u32[]{:S(2)}, u32[]{:S(2)}) async-start(bf16[8,2,12288]{2,1,0:T(2,128)(2,1)} %reshape.212), calls=%async_computation.1 | async-start | bytes 786432 | tf_op jit(solution)/shard_map/all_to_all | solution.py:91
  25.7 3.4 collective-permute-start.3
  29.1 4.5 collective-permute-start.2
  34.0 1.0 copy.186
  42.5 1.9 reshape.213
  44.5 2.3 copy.251
  46.8 1.8 reshape.190
  48.6 2.5 all-gather.3.cloned.1.call-done
  51.1 1.4 fusion.27
  52.5 1.3 convolution_add_fusion.31
  58.7 1.3 collective-permute-start.5
  60.0 4.0 collective-permute-start.4
  64.0 28.9 %all-gather.5.cloned.1.call-done = bf16[256,3,3,256]{3,0,2,1:T(8,128)(2,1)} async-done(((bf16[32,3,3,256]{3,0,2,1:T(8,128)(2,1)}), bf16[256,3,3,256]{3,0,2,1:T(8,128)(2,1)}) %all-gather.5.cloned.1.call-update) | async-done | bytes 1179664 | tf_op jit(solution)/shard_map/all_gather | solution.py:78
  92.9 2.4 reverse_bitcast_fusion.1
  95.3 8.4 %collective-permute-start.7 = (bf16[50,1,256]{2,0,1:T(8,128)(2,1)S(1)}, bf16[50,1,256]{2,0,1:T(8,128)(2,1)S(1)}, u32[]{:S(2)}, u32[]{:S(2)}) collective-permute-start(bf16[50,1,256]{2,0,1:T(8,128)(2,1)S(1)} %get-tuple-element.42), channel_id=1, source_target_pairs={{8,0},{16,8},{24,16},{32,24},{40,32},{48,40},{56,48},{64,56},{72,6... | collective-permute-start | bytes 76808 | tf_op jit(solution)/shard_map/ppermute | solution.py:17
  103.7 4.4 collective-permute-start.6
  114.9 1.4 fusion.19
  117.3 1.3 collective-permute-start.9
  118.6 4.6 collective-permute-start.8
  126.8 1.9 copy.234
  129.6 1.9 collective-permute-start.11
  131.5 6.5 %collective-permute-start.10 = (bf16[50,1,256]{2,0,1:T(8,128)(2,1)S(1)}, bf16[50,1,256]{2,0,1:T(8,128)(2,1)S(1)}, u32[]{:S(2)}, u32[]{:S(2)}) collective-permute-start(bf16[50,1,256]{2,0,1:T(8,128)(2,1)S(1)} %get-tuple-element.39), channel_id=1, source_target_pairs={{0,8},{8,16},{16,24},{24,32},{32,40},{40,48},{48,56},{56,64},{64,7... | collective-permute-start | bytes 76808 | tf_op jit(solution)/shard_map/ppermute | solution.py:14
  138.0 1.0 pad_maximum_fusion.6
  139.3 1.1 pad_maximum_fusion.2
  145.7 1.0 fusion.20
  152.9 2.0 copy.233
  155.5 1.3 collective-permute-start.13
  156.8 4.6 collective-permute-start.12
  161.5 2.0 copy.206
  163.4 2.3 reshape.210
  165.7 4.5 all-to-all-start
  171.0 1.9 collective-permute-start.15
  172.9 6.3 %collective-permute-start.14 = (bf16[50,1,256]{2,0,1:T(8,128)(2,1)S(1)}, bf16[50,1,256]{2,0,1:T(8,128)(2,1)S(1)}, u32[]{:S(2)}, u32[]{:S(2)}) collective-permute-start(bf16[50,1,256]{2,0,1:T(8,128)(2,1)S(1)} %get-tuple-element.35), channel_id=1, source_target_pairs={{0,8},{8,16},{16,24},{24,32},{32,40},{40,48},{48,56},{56,64},{64,7... | collective-permute-start | bytes 76808 | tf_op jit(solution)/shard_map/ppermute | solution.py:14
  179.2 1.0 pad_maximum_fusion.4
  180.5 1.1 pad_maximum_fusion.3
  186.0 34.4 %reduce-scatter.3.cloned.1.call-done = f32[32,3,3,256]{3,0,2,1:T(8,128)} async-done(((f32[256,3,3,256]{3,0,2,1:T(8,128)}), f32[32,3,3,256]{3,0,2,1:T(8,128)}) %reduce-scatter.3.cloned.1.call-update) | async-done | bytes 294928 | tf_op jit(solution)/shard_map/reduce_scatter | solution.py:102
  221.2 1.0 fusion
  222.2 2.3 reshape.211
  224.4 1.2 copy.208
  225.7 1.5 all_to_all.23
  227.1 260.3 %all-reduce.3.cloned.1.call-done = (f32[32,3,3,256]{3,0,2,1:T(8,128)}, f32[32,3,3,256]{3,0,2,1:T(8,128)}) async-done(((f32[32,3,3,256]{3,0,2,1:T(8,128)}, f32[32,3,3,256]{3,0,2,1:T(8,128)}), (f32[32,3,3,256]{3,0,2,1:T(8,128)}, f32[32,3,3,256]{3,0,2,1:T(8,128)})) %all-reduce.3.cloned.1.call-update) | async-done | bytes 589840 | tf_op jit(solution)/shard_map/psum | solution.py:105
  487.5 1.7 copy.270
  489.2 1.7 copy.271
  (185 shorter events, 44.2 us)
Async XLA Ops:
  7.2 7.9 %copy-start.24 = (bf16[32,16,384]{2,1,0:T(8,128)(2,1)S(1)}, bf16[32,16,384]{2,1,0:T(8,128)(2,1)}, u32[]{:S(2)}) copy-start(bf16[32,16,384]{2,1,0:T(8,128)(2,1)} %param.7) | copy-start | bytes 1179652
  7.2 43.9 %all-gather.3.cloned.1.call-start = ((), (), s32[]{:S(2)}) async-start(), calls=%async_computation.4 | async-start | bytes 1327104 | tf_op jit(solution)/shard_map/all_gather | solution.py:77
  9.1 16.6 %collective-permute-start.1 = (bf16[1,16,256]{2,0,1:T(2,128)(2,1)S(1)}, bf16[1,16,256]{2,0,1:T(2,128)(2,1)S(1)}, u32[]{:S(2)}, u32[]{:S(2)}) collective-permute-start(bf16[1,16,256]{2,0,1:T(2,128)(2,1)S(1)} %get-tuple-element.63), channel_id=1, source_target_pairs={{1,0},{2,1},{3,2},{4,3},{5,4},{6,5},{7,6},{9,8},{10,9},{11,10},{12... | collective-permute-start | bytes 24584 | tf_op jit(solution)/shard_map/ppermute | solution.py:17
  10.4 15.3 %collective-permute-start = (bf16[1,16,256]{2,0,1:T(2,128)(2,1)S(1)}, bf16[1,16,256]{2,0,1:T(2,128)(2,1)S(1)}, u32[]{:S(2)}, u32[]{:S(2)}) collective-permute-start(bf16[1,16,256]{2,0,1:T(2,128)(2,1)S(1)} %get-tuple-element.62), channel_id=1, source_target_pairs={{0,1},{1,2},{2,3},{3,4},{4,5},{5,6},{6,7},{8,9},{9,10},{10,11},{11... | collective-permute-start | bytes 24584 | tf_op jit(solution)/shard_map/ppermute | solution.py:14
  18.6 24.0 %all-to-all-start.1 = ((bf16[8,2,12288]{2,1,0:T(2,128)(2,1)}), bf16[8,2,12288]{2,1,0:T(2,128)(2,1)S(1)}, u32[]{:S(2)}, u32[]{:S(2)}) async-start(bf16[8,2,12288]{2,1,0:T(2,128)(2,1)} %reshape.212), calls=%async_computation.1 | async-start | bytes 786432 | tf_op jit(solution)/shard_map/all_to_all | solution.py:91
  24.8 68.0 %all-gather.5.cloned.1.call-start = ((), (), s32[]{:S(2)}) async-start(), calls=%async_computation.5 | async-start | bytes 1327104 | tf_op jit(solution)/shard_map/all_gather | solution.py:78
  25.6 160.4 %reduce-scatter.5.cloned.1.call-start = ((), (), s32[]{:S(2)}) async-start(), calls=%async_computation.7 | async-start | bytes 2654208 | tf_op jit(solution)/shard_map/reduce_scatter | solution.py:103
  25.7 10.2 %collective-permute-start.3 = (bf16[50,1,256]{2,0,1:T(8,128)(2,1)S(1)}, bf16[50,1,256]{2,0,1:T(8,128)(2,1)S(1)}, u32[]{:S(2)}, u32[]{:S(2)}) collective-permute-start(bf16[50,1,256]{2,0,1:T(8,128)(2,1)S(1)} %get-tuple-element.46), channel_id=1, source_target_pairs={{8,0},{16,8},{24,16},{32,24},{40,32},{48,40},{56,48},{64,56},{72,6... | collective-permute-start | bytes 76808 | tf_op jit(solution)/shard_map/ppermute | solution.py:17
  29.1 6.8 %collective-permute-start.2 = (bf16[50,1,256]{2,0,1:T(8,128)(2,1)S(1)}, bf16[50,1,256]{2,0,1:T(8,128)(2,1)S(1)}, u32[]{:S(2)}, u32[]{:S(2)}) collective-permute-start(bf16[50,1,256]{2,0,1:T(8,128)(2,1)S(1)} %get-tuple-element.47), channel_id=1, source_target_pairs={{0,8},{8,16},{16,24},{24,32},{32,40},{40,48},{48,56},{56,64},{64,7... | collective-permute-start | bytes 76808 | tf_op jit(solution)/shard_map/ppermute | solution.py:14
  34.0 1.9 copy-start.22
  34.0 2.3 copy-start.20
  36.2 0.8 copy-start
  36.3 1.1 copy-start.2
  51.1 1.5 copy-start.4
  52.5 1.4 copy-start.19
  53.9 1.0 copy-start.18
  54.2 1.0 copy-start.11
  55.2 1.0 copy-start.17
  55.5 1.0 copy-start.16
  56.9 1.0 copy-start.15
  58.7 36.6 %collective-permute-start.5 = (bf16[1,16,256]{2,0,1:T(2,128)(2,1)S(1)}, bf16[1,16,256]{2,0,1:T(2,128)(2,1)S(1)}, u32[]{:S(2)}, u32[]{:S(2)}) collective-permute-start(bf16[1,16,256]{2,0,1:T(2,128)(2,1)S(1)} %get-tuple-element.59), channel_id=1, source_target_pairs={{1,0},{2,1},{3,2},{4,3},{5,4},{6,5},{7,6},{9,8},{10,9},{11,10},{12... | collective-permute-start | bytes 24584 | tf_op jit(solution)/shard_map/ppermute | solution.py:17
  60.0 35.3 %collective-permute-start.4 = (bf16[1,16,256]{2,0,1:T(2,128)(2,1)S(1)}, bf16[1,16,256]{2,0,1:T(2,128)(2,1)S(1)}, u32[]{:S(2)}, u32[]{:S(2)}) collective-permute-start(bf16[1,16,256]{2,0,1:T(2,128)(2,1)S(1)} %get-tuple-element.58), channel_id=1, source_target_pairs={{0,1},{1,2},{2,3},{3,4},{4,5},{5,6},{6,7},{8,9},{9,10},{10,11},{11... | collective-permute-start | bytes 24584 | tf_op jit(solution)/shard_map/ppermute | solution.py:14
  95.3 13.4 %collective-permute-start.7 = (bf16[50,1,256]{2,0,1:T(8,128)(2,1)S(1)}, bf16[50,1,256]{2,0,1:T(8,128)(2,1)S(1)}, u32[]{:S(2)}, u32[]{:S(2)}) collective-permute-start(bf16[50,1,256]{2,0,1:T(8,128)(2,1)S(1)} %get-tuple-element.42), channel_id=1, source_target_pairs={{8,0},{16,8},{24,16},{32,24},{40,32},{48,40},{56,48},{64,56},{72,6... | collective-permute-start | bytes 76808 | tf_op jit(solution)/shard_map/ppermute | solution.py:17
  103.7 5.2 %collective-permute-start.6 = (bf16[50,1,256]{2,0,1:T(8,128)(2,1)S(1)}, bf16[50,1,256]{2,0,1:T(8,128)(2,1)S(1)}, u32[]{:S(2)}, u32[]{:S(2)}) collective-permute-start(bf16[50,1,256]{2,0,1:T(8,128)(2,1)S(1)} %get-tuple-element.43), channel_id=1, source_target_pairs={{0,8},{8,16},{16,24},{24,32},{32,40},{40,48},{48,56},{56,64},{64,7... | collective-permute-start | bytes 76808 | tf_op jit(solution)/shard_map/ppermute | solution.py:14
  109.2 1.3 copy-start.7
  113.8 1.1 copy-start.10
  117.3 11.5 %collective-permute-start.9 = (bf16[1,16,256]{2,0,1:T(2,128)(2,1)}, bf16[1,16,256]{2,0,1:T(2,128)(2,1)S(1)}, u32[]{:S(2)}, u32[]{:S(2)}) collective-permute-start(bf16[1,16,256]{2,0,1:T(2,128)(2,1)} %get-tuple-element.55), channel_id=1, source_target_pairs={{1,0},{2,1},{3,2},{4,3},{5,4},{6,5},{7,6},{9,8},{10,9},{11,10},{12... | collective-permute-start | bytes 24584 | tf_op jit(solution)/shard_map/ppermute | solution.py:17
  118.6 10.2 %collective-permute-start.8 = (bf16[1,16,256]{2,0,1:T(2,128)(2,1)}, bf16[1,16,256]{2,0,1:T(2,128)(2,1)}, u32[]{:S(2)}, u32[]{:S(2)}) collective-permute-start(bf16[1,16,256]{2,0,1:T(2,128)(2,1)} %get-tuple-element.54), channel_id=1, source_target_pairs={{0,1},{1,2},{2,3},{3,4},{4,5},{5,6},{6,7},{8,9},{9,10},{10,11},{11... | collective-permute-start | bytes 24584 | tf_op jit(solution)/shard_map/ppermute | solution.py:14
  128.8 91.7 %reduce-scatter.3.cloned.1.call-start = ((), (), s32[]{:S(2)}) async-start(), calls=%async_computation.6 | async-start | bytes 2654208 | tf_op jit(solution)/shard_map/reduce_scatter | solution.py:102
  129.6 9.7 %collective-permute-start.11 = (bf16[50,1,256]{2,0,1:T(8,128)(2,1)S(1)}, bf16[50,1,256]{2,0,1:T(8,128)(2,1)S(1)}, u32[]{:S(2)}, u32[]{:S(2)}) collective-permute-start(bf16[50,1,256]{2,0,1:T(8,128)(2,1)S(1)} %get-tuple-element.38), channel_id=1, source_target_pairs={{8,0},{16,8},{24,16},{32,24},{40,32},{48,40},{56,48},{64,56},{72,6... | collective-permute-start | bytes 76808 | tf_op jit(solution)/shard_map/ppermute | solution.py:17
  131.5 7.8 %collective-permute-start.10 = (bf16[50,1,256]{2,0,1:T(8,128)(2,1)S(1)}, bf16[50,1,256]{2,0,1:T(8,128)(2,1)S(1)}, u32[]{:S(2)}, u32[]{:S(2)}) collective-permute-start(bf16[50,1,256]{2,0,1:T(8,128)(2,1)S(1)} %get-tuple-element.39), channel_id=1, source_target_pairs={{0,8},{8,16},{16,24},{24,32},{32,40},{40,48},{48,56},{56,64},{64,7... | collective-permute-start | bytes 76808 | tf_op jit(solution)/shard_map/ppermute | solution.py:14
  141.1 1.4 copy-start.6
  143.3 1.0 copy-start.13
  145.7 1.6 copy-start.8
  145.7 1.3 copy-start.3
  147.0 1.0 copy-start.23
  148.0 1.0 copy-start.1
  149.3 1.0 copy-start.12
  151.0 1.0 copy-start.21
  154.8 6.5 %copy-start.5 = (bf16[256,3,3,256]{3,0,2,1:T(8,128)(2,1)S(1)}, bf16[256,3,3,256]{3,0,2,1:T(8,128)(2,1)}, u32[]{:S(2)}) copy-start(bf16[256,3,3,256]{3,0,2,1:T(8,128)(2,1)} %all-gather.3.cloned.1.call-done) | copy-start | bytes 3538948
  155.5 14.8 %collective-permute-start.13 = (bf16[1,16,256]{2,0,1:T(2,128)(2,1)}, bf16[1,16,256]{2,0,1:T(2,128)(2,1)S(1)}, u32[]{:S(2)}, u32[]{:S(2)}) collective-permute-start(bf16[1,16,256]{2,0,1:T(2,128)(2,1)} %get-tuple-element.51), channel_id=1, source_target_pairs={{1,0},{2,1},{3,2},{4,3},{5,4},{6,5},{7,6},{9,8},{10,9},{11,10},{12... | collective-permute-start | bytes 24584 | tf_op jit(solution)/shard_map/ppermute | solution.py:17
  156.8 13.5 %collective-permute-start.12 = (bf16[1,16,256]{2,0,1:T(2,128)(2,1)}, bf16[1,16,256]{2,0,1:T(2,128)(2,1)}, u32[]{:S(2)}, u32[]{:S(2)}) collective-permute-start(bf16[1,16,256]{2,0,1:T(2,128)(2,1)} %get-tuple-element.50), channel_id=1, source_target_pairs={{0,1},{1,2},{2,3},{3,4},{4,5},{5,6},{6,7},{8,9},{9,10},{10,11},{11... | collective-permute-start | bytes 24584 | tf_op jit(solution)/shard_map/ppermute | solution.py:14
  165.7 56.5 %all-to-all-start = ((bf16[8,2,12288]{2,1,0:T(2,128)(2,1)}), bf16[8,2,12288]{2,1,0:T(2,128)(2,1)}, u32[]{:S(2)}, u32[]{:S(2)}) async-start(bf16[8,2,12288]{2,1,0:T(2,128)(2,1)} %reshape.210), calls=%async_computation | async-start | bytes 786432 | tf_op jit(solution)/shard_map/all_to_all | solution.py:90
  170.2 317.2 %all-reduce.3.cloned.1.call-start = ((), (), s32[]{:S(2)}) async-start(), calls=%async_computation.8 | async-start | bytes 1179648 | tf_op jit(solution)/shard_map/psum | solution.py:105
  171.0 9.5 %collective-permute-start.15 = (bf16[50,1,256]{2,0,1:T(8,128)(2,1)S(1)}, bf16[50,1,256]{2,0,1:T(8,128)(2,1)S(1)}, u32[]{:S(2)}, u32[]{:S(2)}) collective-permute-start(bf16[50,1,256]{2,0,1:T(8,128)(2,1)S(1)} %get-tuple-element.34), channel_id=1, source_target_pairs={{8,0},{16,8},{24,16},{32,24},{40,32},{48,40},{56,48},{64,56},{72,6... | collective-permute-start | bytes 76808 | tf_op jit(solution)/shard_map/ppermute | solution.py:17
  172.9 7.6 %collective-permute-start.14 = (bf16[50,1,256]{2,0,1:T(8,128)(2,1)S(1)}, bf16[50,1,256]{2,0,1:T(8,128)(2,1)S(1)}, u32[]{:S(2)}, u32[]{:S(2)}) collective-permute-start(bf16[50,1,256]{2,0,1:T(8,128)(2,1)S(1)} %get-tuple-element.35), channel_id=1, source_target_pairs={{0,8},{8,16},{16,24},{24,32},{32,40},{40,48},{48,56},{56,64},{64,7... | collective-permute-start | bytes 76808 | tf_op jit(solution)/shard_map/ppermute | solution.py:14
  184.1 1.1 copy-start.9
  185.7 34.8 %copy-start.14 = (bf16[48,16,256]{2,1,0:T(8,128)(2,1)S(1)}, bf16[48,16,256]{2,1,0:T(8,128)(2,1)}, u32[]{:S(2)}) copy-start(bf16[48,16,256]{2,1,0:T(8,128)(2,1)} %copy.228) | copy-start | bytes 1179652
Sparse Core Ops, SparseCore 0:
  9.8 41.2 all-gather.2
  52.9 39.9 all-gather.4
  128.9 42.8 reduce-scatter.4
  174.2 46.2 reduce-scatter.2
  223.0 264.4 all-reduce.2
where the time goes:
time: 500 us; the launch traced here: 497 us
  waiting for transfers between devices  329 us (66%)
  starting transfers between devices  71.3 us (14%)
  local copies, waits for them, and re-layouts  53.5 us (11%)
  matrix products  18.7 us (4%)
  between operations  14.9 us (3%)
  other arithmetic  10.3 us (2%)
    psum x1, waiting for transfers between devices, body(): first_grad, second_grad = lax.psum((first_part, second_part), 'gx')  260 us
    ppermute x8, starting transfers between devices, padded_2(): lax.ppermute(lax.slice_in_dim(block, block.shape[dim] - width, None, axis...  39.5 us
    reduce_scatter x1, waiting for transfers between devices, body(): lax.psum_scatter(from_taps(first_local), 'gy', scatter_dimension=0, tiled...  34.4 us
    all_gather x1, waiting for transfers between devices, body(): lax.all_gather(second_filter, 'gy', axis=0, tiled=True)  28.9 us
    unnamed x58, local copies, waits for them, and re-layouts  24.5 us
    ppermute x8, starting transfers between devices, padded_2(): lax.ppermute(lax.slice_in_dim(block, 0, width, axis=dim), axis, backward)  20.8 us
    dot_general x36, matrix products, conv_taps(): jnp.dot(window, weight[i, j], preferred_element_type=jnp.float32)  13.1 us
    slice x39, local copies, waits for them, and re-layouts, conv_taps(): padded[i:i + height, j:j + width, :]  11.8 us
  transfers between devices with their start and end apart: 23, of which 6 were waited for; matrix products, arithmetic and copies ran while one was open for 12% of the time, Pallas kernels for 0%

commit v1 on v0

v1 whole, which is shorter than its diff:
```python
import functools
import math

import jax
import jax.numpy as jnp
from jax import lax
from jax.experimental import pallas as pl
from jax.experimental.pallas import tpu as pltpu
from jax.sharding import PartitionSpec as P

MESH = pl.DeviceIdType.MESH
F32 = jnp.float32
BF16 = jnp.bfloat16

CH = 256
RB = 48
CB = 16
ST = 64
LANES = 9 * CH
HALF = LANES // 2
PIECE = 384
NGX = 32
NGY = 8

NT = (((1,), (1,)), ((), ()))
NN = (((1,), (0,)), ((), ()))


def mm(a, b, dims):
    return lax.dot_general(a, b, dims, preferred_element_type=F32)


def place(x, y, z, core):
    xw, yw, zw = lax.rem(x + 8, 4), lax.rem(y + 8, 4), lax.rem(z + 16, 8)
    xh = lax.div(xw, 2)
    return {"gx": zw * 4 + xh * 2 + core, "gy": (xw - 2 * xh) * 4 + yw}


def kernel(
    scale,
    feat, w1, w2, cot,
    out_o, ig_o, g1_o, g2_o,
    f32a, p32, fs, pre1, sl1, h32, hs, cott, sendc, sel1, bmat, outs, rout, otb, o32t, o32, os_, i32, imt, is_,
    ig32, amat, sel2, out32, wg, colbuf, rc, rr, t32,
    gf, gb, rb, sb, rx, tz, rz, fin, finp,
    sy, ry, sx, rxs, sc, rcs, sh, rh, scot, rcot, so, ro, sp, rp, spl, rpl, sz, rzs, sg, rg, sf, rf,
):
    gx = lax.axis_index("gx")
    gy = lax.axis_index("gy")
    core = lax.rem(gx, 2)
    xh = lax.rem(lax.div(gx, 2), 2)
    z = lax.div(gx, 4)
    y = lax.rem(gy, 4)
    xl = lax.div(gy, 4)
    x = xh * 2 + xl
    gxl, gxr = lax.rem(gx + NGX - 1, NGX), lax.rem(gx + 1, NGX)
    partner = {"gx": gx + 1 - 2 * core, "gy": gy}

    def at_gy(d, column=None):
        return {"gx": gx if column is None else column, "gy": lax.rem(gy + d, NGY)}

    def rcopy(src, dst, ssem, rsem, dev):
        return pltpu.make_async_remote_copy(
            src_ref=src, dst_ref=dst, send_sem=ssem, recv_sem=rsem, device_id=dev, device_id_type=MESH
        )

    barrier = pltpu.get_barrier_semaphore()
    peers = [at_gy(d) for d in range(1, NGY)]
    peers += [at_gy(d, side) for side in (gxl, gxr) for d in range(NGY)]
    peers += [at_gy(d, z * 4 + (1 - xh) * 2 + core) for d in range(NGY)]
    peers += [place(x + 2 * dxh, y, z + dz, core) for dz in range(1, 8) for dxh in range(2)]
    for peer in peers:
        pl.semaphore_signal(barrier, inc=1, device_id=peer, device_id_type=MESH)
    pl.semaphore_wait(barrier, len(peers))

    pending = []

    def go(copy):
        copy.start()
        pending.append(copy)
        return copy

    filters = (w1, w2)

    def shard_row(xlo, yy):
        return (xlo * 4 + yy) * 32

    ycopies = {}
    xcopies = {}
    ccopies = {}

    def y_send(f, dy):
        row = pl.multiple_of(shard_row(xl, y) + 16 * core, 16)
        src = filters[f].at[pl.ds(pl.multiple_of(16 * core, 16), 16), :]
        ycopies[f, dy] = go(
            rcopy(src, wg.at[f, pl.ds(row, 16), :], sy.at[f, dy - 1], ry.at[f, dy - 1], place(x, y + dy, z, core))
        )

    def x_send(f, dy):
        row = pl.multiple_of(shard_row(xl, lax.rem(y - dy + 4, 4)) + 16 * core, 16)
        for side in range(2):
            if dy == 0:
                src = filters[f].at[pl.ds(pl.multiple_of(16 * core, 16), 16), pl.ds(side * HALF, HALF)]
            else:
                src = wg.at[f, pl.ds(row, 16), pl.ds(side * HALF, HALF)]
            dst = wg.at[f, pl.ds(row, 16), pl.ds(side * HALF, HALF)]
            xcopies[f, dy, side] = go(
                rcopy(src, dst, sx.at[f, dy, side], rxs.at[f, dy, side], place(x + 1 - 2 * side, y, z, core))
            )

    def c_send(f, other, dy):
        xlo = 1 - xl if other else xl
        row = pl.multiple_of(shard_row(xlo, lax.rem(y - dy + 4, 4)) + 16 * core, 16)
        ref = wg.at[f, pl.ds(row, 16), :]
        ccopies[f, other, dy] = go(rcopy(ref, ref, sc.at[f, other, dy], rcs.at[f, other, dy], partner))

    def filter_start(f):
        for dy in (1, 3, 2):
            y_send(f, dy)
        x_send(f, 0)
        wg[f, pl.ds(pl.multiple_of(shard_row(xl, y), 32), 32), :] = filters[f][...]

    def filter_pass(f):
        for dy in (1, 3, 2):
            ycopies[f, dy].wait_recv()
            x_send(f, dy)
            c_send(f, 0, dy)
        for dy in (0, 1, 3, 2):
            for side in range(2):
                xcopies[f, dy, side].wait_recv()
            c_send(f, 1, dy)

    def filter_end(f):
        for dy in (1, 3, 2):
            ccopies[f, 0, dy].wait_recv()
        for dy in (0, 1, 3, 2):
            ccopies[f, 1, dy].wait_recv()

    def split(ref, value):
        for k in range(value.shape[1] // 128):
            ref[k] = value[:, k * 128:(k + 1) * 128]

    def strided(ref, start, size, stride):
        return jnp.concatenate([ref[k, pl.ds(start, size, stride=stride), :] for k in range(ref.shape[0])], axis=1)

    def put_strided(ref, start, size, stride, value):
        for k in range(ref.shape[0]):
            ref[k, pl.ds(start, size, stride=stride), :] = value[:, k * 128:(k + 1) * 128]

    def joined(ref):
        return jnp.concatenate([ref[k] for k in range(ref.shape[0])], axis=1)

    filter_start(0)

    hcopies = []
    for v, (rows, dg) in enumerate(((RB - 4, 1), (0, NGY - 1))):
        for h, column in enumerate((gxr, None, gxl)):
            hcopies.append(
                go(rcopy(feat.at[pl.ds(rows, 4)], rr.at[v, h], sh.at[v, h], rh.at[v, h], at_gy(dg, column)))
            )
    split(f32a, feat[...].astype(F32).reshape(RB * CB, CH))
    for c in (12, 13, 14, 15, 0, 1, 2, 3):
        colbuf[0 if c > 7 else 1, c % 4] = strided(f32a, c, RB, CB).astype(BF16)
    hcopies.append(go(rcopy(colbuf.at[0], rc.at[0], sh.at[2, 0], rh.at[2, 0], at_gy(0, gxr))))
    hcopies.append(go(rcopy(colbuf.at[1], rc.at[1], sh.at[2, 1], rh.at[2, 1], at_gy(0, gxl))))

    filter_start(1)

    split(out32, cot[...].astype(F32).reshape(32 * CB, 384))
    for c in range(CB):
        bmat[pl.ds((c // 2) * 32, 32), pl.ds((c % 2) * 384, 384)] = strided(out32, c, 32, CB).astype(BF16)
    rows_k = lax.broadcasted_iota(jnp.int32, (768, 128), 0)
    lane = lax.broadcasted_iota(jnp.int32, (1, 128), 1)
    high = jnp.where(lane >= 64, 1, 0)
    for b in range(NGY):
        row_of = 48 * b - 8 + lane - 64 * high
        target = jnp.where((row_of >= 0) & (row_of < 384), row_of + 384 * high, -1)
        sel1[...] = jnp.where(rows_k == target, 1.0, 0.0).astype(BF16)
        res = mm(bmat[...], sel1[...], NN).astype(BF16)
        for cp in range(8):
            sendc[b, :, pl.ds(cp * 128, 128)] = res[cp * 32:(cp + 1) * 32, :]
    row = pl.multiple_of(gy * 32, 32)
    cotcopies = []
    for d in range(1, NGY):
        dev = at_gy(d)
        cotcopies.append(
            go(rcopy(sendc.at[dev["gy"]], cott.at[pl.ds(row, 32), pl.ds(128, 1024)], scot.at[0, d], rcot.at[0, d], dev))
        )
    for d in range(NGY):
        for side, column in ((1, gxr), (2, gxl)):
            dev = at_gy(d, column)
            src = sendc.at[dev["gy"], :, pl.ds(896 if side == 1 else 0, 128)]
            dst = cott.at[pl.ds(row, 32), pl.ds(0 if side == 1 else 1152, 128)]
            cotcopies.append(go(rcopy(src, dst, scot.at[side, d], rcot.at[side, d], dev)))
    cott[pl.ds(row, 32), pl.ds(128, 1024)] = sendc[gy]

    filter_pass(0)

    p32[...] = jnp.zeros_like(p32)
    for c in range(CB):
        p32[pl.ds(8 + (4 + c) * ST + 8, RB), :] = strided(f32a, c, RB, CB)
    for copy in hcopies:
        copy.wait_recv()
    in_left = jnp.where(gx > 0, 1.0, 0.0)
    in_right = jnp.where(gx < NGX - 1, 1.0, 0.0)
    in_up = jnp.where(gy > 0, 1.0, 0.0)
    in_down = jnp.where(gy < NGY - 1, 1.0, 0.0)
    for c in range(4):
        p32[pl.ds(8 + c * ST + 8, RB), :] = rc[0, c].astype(F32) * in_left
        p32[pl.ds(8 + (20 + c) * ST + 8, RB), :] = rc[1, c].astype(F32) * in_right
    for v, in_v in enumerate((in_up, in_down)):
        for h, in_h in enumerate((in_left, 1.0, in_right)):
            split(t32.at[v, h], rr[v, h].astype(F32).reshape(64, CH) * (in_v * in_h))
            for c in range(CB):
                col = (c - 12, c + 4, c + 20)[h]
                if 0 <= col < 24:
                    p32[pl.ds(8 + col * ST + (4 if v == 0 else 56), 4), :] = strided(t32.at[v, h], c, 4, CB)

    def shifts(src, dst, count):
        for d in range(3):
            dst[:, pl.ds(d * CH, CH)] = src[pl.ds(7 + d, count), :].astype(BF16)

    shifts(p32, fs, 24 * ST)
    filter_end(0)

    def tap(f, i, j):
        return wg[f, :, pl.ds((i * 3 + j) * CH, CH)]

    def taps_in(f, j):
        return jnp.concatenate([tap(f, i, j) for i in range(3)], axis=1)

    def taps_out(f, j):
        return jnp.concatenate([tap(f, 2 - i, j) for i in range(3)], axis=0)

    for t in range(2):
        acc = None
        for j in range(3):
            term = mm(fs[pl.ds(j * ST + t * 704, 704), :], taps_in(0, j), NT)
            acc = term if acc is None else acc + term
        pre1[pl.ds(t * 704, 704), :] = acc

    filter_pass(1)

    row_in = lax.broadcasted_iota(jnp.int32, (ST, CH), 0) + (48 * gy - 8)
    rows_ok = (row_in >= 0) & (row_in < 384)
    rows_ok_f = jnp.where(rows_ok, 1.0, 0.0)
    h32[pl.ds(0, 8), :] = jnp.zeros((8, CH), F32)
    h32[pl.ds(8 + 22 * ST, 8), :] = jnp.zeros((8, CH), F32)

    @pl.loop(0, 22)
    def _(c):
        at = pl.multiple_of(c * ST, ST)
        v = pre1[pl.ds(at, ST), :]
        s = 1.0 / (1.0 + jnp.exp(-v))
        col = 16 * gx + c - 3
        ok = jnp.where((col >= 0) & (col < 512), 1.0, 0.0)
        h32[pl.ds(at + 8, ST), :] = v * s * (rows_ok_f * ok)
        sl1[pl.ds(at, ST), :] = s * (1.0 + v * (1.0 - s))

    shifts(h32, hs, 22 * ST)
    filter_end(1)
    for copy in cotcopies:
        copy.wait_recv()

    lane2 = lax.broadcasted_iota(jnp.int32, (CH, 256), 1)
    in_block = jnp.where(((lane2 & 63) >= 8) & ((lane2 & 63) < 56), 1.0, 0.0)
    for t in range(5):
        acc = None
        for j in range(3):
            term = mm(taps_in(1, j), hs[pl.ds(j * ST + t * 256, 256), :], NT)
            acc = term if acc is None else acc + term
        s = 1.0 / (1.0 + jnp.exp(-acc))
        act = (acc * s).astype(BF16).reshape(NGY, 32, 256)
        outer = cott[:, pl.ds(t * 256, 256)].astype(F32) * (s * (1.0 + acc * (1.0 - s)))
        if t == 0:
            outer = jnp.where((lane2 >= 128) | (gx > 0), outer, 0.0)
        if t == 4:
            outer = jnp.where((lane2 < 128) | (gx < NGX - 1), outer, 0.0)
        o32t[:, pl.ds(t * 256, 256)] = outer
        own = (outer * in_block).astype(BF16)
        lo, hi = (128 if t == 0 else 0), (128 if t == 4 else 256)
        outs[:, :, pl.ds(t * 256 + lo - 128, hi - lo)] = act[:, :, lo:hi]
        otb[:, pl.ds(t * 256 + lo - 128, hi - lo)] = own[:, lo:hi]

    outcopies = []
    for d in range(1, NGY):
        dev = at_gy(d)
        outcopies.append(go(rcopy(outs.at[dev["gy"]], rout.at[gy], so.at[d], ro.at[d], dev)))
    rout[gy] = outs[gy]

    def grad(g, left, right, base):
        for j in range(3):
            part = mm(left[...], right[pl.ds((base + j) * ST, 1024), :], NN)
            for i in range(3):
                value = part[:, i * CH:(i + 1) * CH].reshape(8, 2, 16, CH)
                gf[g, :, :, :, pl.ds((i * 3 + j) * CH, CH)] = value
                gb[g, :, :, :, pl.ds((i * 3 + j) * CH, CH)] = value.astype(BF16)
        return go(rcopy(gb.at[g, :, 1 - core], rb.at[g], sp.at[g], rp.at[g], partner))

    def plane(g, pair):
        pair.wait_recv()

        @pl.loop(0, NGY)
        def _(b):
            for k in range(2):
                part = gf[g, b, core, :, pl.ds(k * HALF, HALF)] + rb[g, b, :, pl.ds(k * HALF, HALF)].astype(F32)
                sb[g, b, k] = part.astype(BF16)

        copies = []
        for dx, dy in ((1, 0), (3, 0), (0, 1), (0, 3), (1, 1), (3, 3), (1, 3), (3, 1), (2, 0), (0, 2), (2, 1), (1, 2), (2, 3), (3, 2), (2, 2)):
            tx = lax.rem(x + dx, 4)
            dev = place(x + dx, y + dy, z, core)
            slot = dx * 4 + dy
            copies.append(
                go(rcopy(sb.at[g, dev["gy"], lax.div(tx, 2)], rx.at[g, slot], spl.at[g, slot], rpl.at[g, slot], dev))
            )
        return copies

    pair2 = grad(1, otb, hs, 2)

    o32[pl.ds(0, 8), :] = jnp.zeros((8, CH), F32)
    o32[pl.ds(8 + 20 * ST, 8), :] = jnp.zeros((8, CH), F32)
    for t in range(5):
        o32[pl.ds(8 + t * 256, 256), :] = o32t[:, pl.ds(t * 256, 256)].T
    shifts(o32, os_, 20 * ST)

    plane2 = plane(1, pair2)

    i32[pl.ds(0, 8), :] = jnp.zeros((8, CH), F32)
    i32[pl.ds(8 + 18 * ST, 8), :] = jnp.zeros((8, CH), F32)
    for t in range(2):
        acc = None
        for j in range(3):
            term = mm(os_[pl.ds((2 - j) * ST + t * 576, 576), :], taps_out(1, j), NN)
            acc = term if acc is None else acc + term
        i32[pl.ds(8 + t * 576, 576), :] = acc

    @pl.loop(0, 18)
    def _(c):
        at = pl.multiple_of(c * ST, ST)
        col = 16 * gx + c - 1
        ok = jnp.where((col >= 0) & (col < 512), 1.0, 0.0)
        i32[pl.ds(at + 8, ST), :] = i32[pl.ds(at + 8, ST), :] * sl1[pl.ds(at + 128, ST), :] * (rows_ok_f * ok)

    for t in range(4):
        imt[:, pl.ds(t * 256, 256)] = (i32[pl.ds(8 + 64 + t * 256, 256), :].T * in_block).astype(BF16)
    pair1 = grad(0, imt, fs, 3)

    shifts(i32, is_, 18 * ST)
    plane1 = plane(0, pair1)
    acc = None
    for j in range(3):
        term = mm(is_[pl.ds((2 - j) * ST, 1024), :], taps_out(0, j), NN)
        acc = term if acc is None else acc + term
    for c in range(CB):
        put_strided(ig32, c, RB, CB, acc[c * ST + 8:c * ST + 8 + RB, :])
    ig_o[...] = joined(ig32).astype(BF16).reshape(RB, CB, CH)

    for copy in outcopies:
        copy.wait_recv()
    rows_n = lax.broadcasted_iota(jnp.int32, (1024, 384), 0)
    h_lane = lax.broadcasted_iota(jnp.int32, (1, 384), 1)
    band = jnp.zeros((1, 384), jnp.int32)
    for b in range(1, NGY):
        band = band + jnp.where(h_lane >= 48 * b, 1, 0)
    for src in range(NGY):
        for cp in range(8):
            amat[pl.ds(cp * 32, 32), pl.ds(src * 128, 128)] = rout[src, :, pl.ds(cp * 128, 128)]
    for par in range(2):
        target = band * 80 + h_lane + (8 + 64 * par)
        sel2[...] = jnp.where(rows_n == target, 1.0, 0.0).astype(BF16)
        res = mm(amat[...], sel2[...], NN)
        for cp in range(8):
            put_strided(out32, 2 * cp + par, 32, CB, res[cp * 32:(cp + 1) * 32, :])
    out_o[...] = joined(out32).astype(BF16).reshape(32, CB, 384)

    for g, copies in ((1, plane2), (0, plane1)):
        for copy in copies:
            copy.wait_recv()
        for k in range(3):
            lanes = pl.ds(k * PIECE, PIECE)
            total = sb[g, gy, xh, :, lanes].astype(F32)
            for slot in range(1, 16):
                total = total + rx[g, slot, :, lanes].astype(F32)
            tz[g * 3 + k] = total.astype(BF16)
    tz[pl.ds(6, 2)] = jnp.zeros((2, 16, PIECE), BF16)
    zcopies = []
    for dz in (1, 7, 2, 6, 3, 5, 4):
        zt = lax.rem(z + dz, 8)
        zcopies.append(go(rcopy(tz.at[zt], rz.at[dz], sz.at[dz], rzs.at[dz], place(x, y, z + dz, core))))
    for copy in zcopies:
        copy.wait_recv()
    total = tz[z].astype(F32)
    for dz in range(1, 8):
        total = total + rz[dz].astype(F32)
    slot = z * 2 + xh
    fin[slot] = total.astype(BF16)
    gcopies = []
    for dz in range(8):
        for dxh in range(2):
            if dz or dxh:
                gcopies.append(
                    go(rcopy(fin.at[slot], fin.at[slot], sg.at[dz, dxh], rg.at[dz, dxh], place(x + 2 * dxh, y, z + dz, core)))
                )
    for copy in gcopies:
        copy.wait_recv()
    last = go(rcopy(fin.at[pl.ds(0, 12)], finp, sf, rf, partner))
    mine = pl.multiple_of(16 * core, 16)
    theirs = pl.multiple_of(16 - 16 * core, 16)
    outs_g = (g1_o, g2_o)
    for q in range(12):
        lanes = pl.ds((q % 2) * HALF + ((q // 2) % 3) * PIECE, PIECE)
        outs_g[q // 6][pl.ds(mine, 16), lanes] = fin[q].astype(F32) * scale
    last.wait_recv()
    for q in range(12):
        lanes = pl.ds((q % 2) * HALF + ((q // 2) % 3) * PIECE, PIECE)
        outs_g[q // 6][pl.ds(theirs, 16), lanes] = finp[q].astype(F32) * scale
    for copy in pending:
        copy.wait_send()


def solution(mesh):
    scale = 1.0 / math.sqrt(384 * 512)
    vm = pltpu.VMEM
    dma = pltpu.SemaphoreType.DMA
    scratch = [
        vm((2, 768, 128), F32),
        vm((24 * ST + 16, CH), F32),
        vm((24 * ST, 768), BF16),
        vm((22 * ST, CH), F32),
        vm((22 * ST, CH), F32),
        vm((22 * ST + 16, CH), F32),
        vm((22 * ST, 768), BF16),
        vm((CH, 1280), BF16),
        vm((8, 32, 1024), BF16),
        vm((768, 128), BF16),
        vm((256, 768), BF16),
        vm((8, 32, 1024), BF16),
        vm((8, 32, 1024), BF16),
        vm((CH, 1024), BF16),
        vm((CH, 1280), F32),
        vm((20 * ST + 16, CH), F32),
        vm((20 * ST, 768), BF16),
        vm((18 * ST + 16, CH), F32),
        vm((CH, 1024), BF16),
        vm((18 * ST, 768), BF16),
        vm((2, 768, 128), F32),
        vm((256, 1024), BF16),
        vm((1024, 384), BF16),
        vm((3, 512, 128), F32),
        vm((2, CH, LANES), BF16),
        vm((2, 4, RB, CH), BF16),
        vm((2, 4, RB, CH), BF16),
        vm((2, 3, 4, 16, CH), BF16),
        vm((2, 3, 2, 64, 128), F32),
        vm((2, 8, 2, 16, LANES), F32),
        vm((2, 8, 2, 16, LANES), BF16),
        vm((2, 8, 16, LANES), BF16),
        vm((2, 8, 2, 16, HALF), BF16),
        vm((2, 16, 16, HALF), BF16),
        vm((8, 16, PIECE), BF16),
        vm((8, 16, PIECE), BF16),
        vm((16, 16, PIECE), BF16),
        vm((12, 16, PIECE), BF16),
        dma((2, 3)), dma((2, 3)),
        dma((2, 4, 2)), dma((2, 4, 2)),
        dma((2, 2, 4)), dma((2, 2, 4)),
        dma((3, 3)), dma((3, 3)),
        dma((3, 8)), dma((3, 8)),
        dma((8,)), dma((8,)),
        dma((2,)), dma((2,)),
        dma((2, 16)), dma((2, 16)),
        dma((8,)), dma((8,)),
        dma((8, 2)), dma((8, 2)),
        dma, dma,
    ]
    call = pl.pallas_call(
        functools.partial(kernel, scale),
        name="step",
        out_shape=(
            jax.ShapeDtypeStruct((32, CB, 384), BF16),
            jax.ShapeDtypeStruct((RB, CB, CH), BF16),
            jax.ShapeDtypeStruct((32, LANES), F32),
            jax.ShapeDtypeStruct((32, LANES), F32),
        ),
        in_specs=[pl.BlockSpec(memory_space=pltpu.VMEM)] * 4,
        out_specs=[pl.BlockSpec(memory_space=pltpu.VMEM)] * 4,
        scratch_shapes=scratch,
        compiler_params=pltpu.CompilerParams(
            collective_id=0, has_side_effects=True, vmem_limit_bytes=60 * 1024 * 1024
        ),
    )

    def body(features, first_filter, second_filter, cotangent):
        out, ig, g1, g2 = call(
            features, first_filter.reshape(32, LANES), second_filter.reshape(32, LANES), cotangent
        )
        return out, ig, g1.reshape(32, 3, 3, CH), g2.reshape(32, 3, 3, CH)

    in_specs = (
        P("gy", "gx", None),
        P("gy", None, None, None),
        P("gy", None, None, None),
        P("gy", "gx", None),
    )
    out_specs = (
        P("gy", "gx", None),
        P("gy", "gx", None),
        P("gy", None, None, None),
        P("gy", None, None, None),
    )
    return jax.shard_map(body, mesh=mesh, in_specs=in_specs, out_specs=out_specs, check_vma=False)
```

time: 500 us -> 89.8 us (0.18)
  waiting for transfers between devices: 329 us -> 0 us
  Pallas kernels: 0 us -> 80.7 us
  starting transfers between devices: 71.3 us -> 0 us
  local copies, waits for them, and re-layouts: 53.5 us -> 8.12 us
  matrix products: 18.7 us -> 0 us
  between operations: 14.9 us -> 0.68 us
  other arithmetic: 10.3 us -> 0 us
    psum x1 -> x0, waiting for transfers between devices: 260 us -> none  [body(): first_grad, second_grad = lax.psum((first_part, second_part), 'gx')]
    pallas_call x0 -> x1, Pallas kernels: none -> 80.7 us  [body(): call(features, first_filter.reshape(32, LANES), second_filter.reshape(32,...]
    ppermute x16 -> x0, starting transfers between devices: 60.4 us -> none  [the longest x8 39.5 us: padded_2(): lax.ppermute(lax.slice_in_dim(block, block.shape[dim] - width, None, axis...]
    reduce_scatter x2 -> x0, waiting for transfers between devices: 34.5 us -> none  [the longest x1 34.4 us: body(): lax.psum_scatter(from_taps(first_local), 'gy', scatter_dimension=0, tiled...]
    all_gather x2 -> x0, waiting for transfers between devices: 31.4 us -> none  [the longest x1 28.9 us: body(): lax.all_gather(second_filter, 'gy', axis=0, tiled=True)]
    unnamed x58 -> x14, local copies, waits for them, and re-layouts: 24.5 us -> 5.19 us
    dot_general x54 -> x0, matrix products: 18.7 us -> none  [the longest x36 13.1 us: conv_taps(): jnp.dot(window, weight[i, j], preferred_element_type=jnp.float32)]
    slice x43 -> x0, local copies, waits for them, and re-layouts: 13.1 us -> none  [the longest x39 11.8 us: conv_taps(): padded[i:i + height, j:j + width, :]]
  transfers between devices with their start and end apart: 23 -> 0, of which waited for: 6 -> 0; matrix products, arithmetic and copies ran while one was open for 12% -> 0% of each run, Pallas kernels for 0% -> 0%
where the time goes in v1:
time: 89.8 us; the launch traced here: 89.5 us
  Pallas kernels  80.7 us (90%)
  local copies, waits for them, and re-layouts  8.12 us (9%)
    pallas_call x1, Pallas kernels, body(): call(features, first_filter.reshape(32, LANES), second_filter.reshape(32,...  80.7 us
    unnamed x14, local copies, waits for them, and re-layouts  5.19 us

profile of v1, /device:TPU:1, one launch (start us, length us, event | category | flops | bytes accessed | tf_op | source)
XLA Modules:
  0.0 89.5 jit_solution(7612194491046662090)
XLA Ops:
  0.6 1.0 %copy.12 = bf16[32,3,3,256]{3,2,1,0:T(4,128)(2,1)S(1)} copy(bf16[32,3,3,256]{3,0,2,1:T(8,128)(2,1)} %param.5) | data formatting | bytes 294912 | tf_op args[1]
  1.7 0.0 copy-start.3
  1.7 0.8 reshape.20.w1
  2.5 0.1 copy-done.3
  2.6 0.1 copy.13
  2.7 0.8 reshape.21.w2
  3.5 80.7 %step.1 = (bf16[32,16,384]{2,1,0:T(8,128)(2,1)}, bf16[48,16,256]{2,1,0:T(8,128)(2,1)}, f32[32,2304]{1,0:T(8,128)}, f32[32,2304]{1,0:T(8,128)}) custom-call(bf16[48,16,256]{2,1,0:T(8,128)(2,1)} %feat.1, bf16[32,2304]{1,0:T(8,128)(2,1)} %reshape.20.w1, bf16[32,2304]{1,0:T(8,128)(2,1)} %reshape.21.w2, bf16[32,16,384]{2,1,0:T(8,128)(2,1)} %cot.1), custom_call_target="tpu_custom_call" | custom-call | tf_op jit(solution)/shard_map/step/pallas_call | solution.py:495
  84.2 1.1 %reshape.22 = f32[32,3,3,256]{3,2,1,0:T(4,128)S(1)} reshape(f32[32,2304]{1,0:T(8,128)} %get-tuple-element.10) | data formatting | bytes 589824 | tf_op jit(solution)/shard_map/reshape | solution.py:498
  85.3 0.0 copy-start.2
  85.4 0.8 copy.14
  86.1 0.2 copy-done.2
  86.3 0.2 reshape.23
  86.5 0.0 copy-start.1
  86.5 0.8 copy.15
  87.3 0.3 copy-done.1
  87.6 0.0 copy-start
  87.6 0.7 copy.18
  88.3 0.4 copy-done
  88.7 0.7 copy.19
Async XLA Ops:
  1.7 0.9 %copy-start.3 = (bf16[32,3,3,256]{3,0,2,1:T(8,128)(2,1)S(1)}, bf16[32,3,3,256]{3,0,2,1:T(8,128)(2,1)}, u32[]{:S(2)}) copy-start(bf16[32,3,3,256]{3,0,2,1:T(8,128)(2,1)} %param.6) | copy-start | bytes 442372
  85.3 1.0 %copy-start.2 = (f32[32,2304]{1,0:T(8,128)S(1)}, f32[32,2304]{1,0:T(8,128)}, u32[]{:S(2)}) copy-start(f32[32,2304]{1,0:T(8,128)} %get-tuple-element.11) | copy-start | bytes 884740
  86.5 1.1 %copy-start.1 = (bf16[32,16,384]{2,1,0:T(8,128)(2,1)S(1)}, bf16[32,16,384]{2,1,0:T(8,128)(2,1)}, u32[]{:S(2)}) copy-start(bf16[32,16,384]{2,1,0:T(8,128)(2,1)} %get-tuple-element.24) | copy-start | bytes 1179652
  87.6 1.1 %copy-start = (bf16[48,16,256]{2,1,0:T(8,128)(2,1)S(1)}, bf16[48,16,256]{2,1,0:T(8,128)(2,1)}, u32[]{:S(2)}) copy-start(bf16[48,16,256]{2,1,0:T(8,128)(2,1)} %get-tuple-element.25) | copy-start | bytes 1179652

commit v2 on v1

--- a/solution.py
+++ b/solution.py
@@ -16,9 +16,7 @@
 RB = 48
 CB = 16
 ST = 64
-LANES = 9 * CH
-HALF = LANES // 2
-PIECE = 384
+OWNERS = 5
 NGX = 32
 NGY = 8
 
@@ -38,12 +36,13 @@
 
 def kernel(
     scale,
-    feat, w1, w2, cot,
+    feat_i, w1_i, w2_i, cot_i,
     out_o, ig_o, g1_o, g2_o,
+    feat, w1, w2, cot, outv, igv, gv,
     f32a, p32, fs, pre1, sl1, h32, hs, cott, sendc, sel1, bmat, outs, rout, otb, o32t, o32, os_, i32, imt, is_,
     ig32, amat, sel2, out32, wg, colbuf, rc, rr, t32,
     gf, gb, rb, sb, rx, tz, rz, fin, finp,
-    sy, ry, sx, rxs, sc, rcs, sh, rh, scot, rcot, so, ro, sp, rp, spl, rpl, sz, rzs, sg, rg, sf, rf,
+    sy, ry, sx, rxs, sc, rcs, sh, rh, scot, rcot, so, ro, sp, rp, spl, rpl, sz, rzs, sg, rg, sf, rf, sin, sout,
 ):
     gx = lax.axis_index("gx")
     gy = lax.axis_index("gy")
@@ -64,6 +63,13 @@
             src_ref=src, dst_ref=dst, send_sem=ssem, recv_sem=rsem, device_id=dev, device_id_type=MESH
         )
 
+    loads = [
+        pltpu.make_async_copy(src, dst, sin.at[n])
+        for n, (src, dst) in enumerate(((w1_i, w1), (feat_i, feat), (w2_i, w2), (cot_i, cot)))
+    ]
+    for load in loads:
+        load.start()
+
     barrier = pltpu.get_barrier_semaphore()
     peers = [at_gy(d) for d in range(1, NGY)]
     peers += [at_gy(d, side) for side in (gxl, gxr) for d in range(NGY)]
@@ -72,6 +78,7 @@
     for peer in peers:
         pl.semaphore_signal(barrier, inc=1, device_id=peer, device_id_type=MESH)
     pl.semaphore_wait(barrier, len(peers))
+    loads[0].wait()
 
     pending = []
 
@@ -91,19 +98,20 @@
 
     def y_send(f, dy):
         row = pl.multiple_of(shard_row(xl, y) + 16 * core, 16)
-        src = filters[f].at[pl.ds(pl.multiple_of(16 * core, 16), 16), :]
+        src = filters[f].at[:, pl.ds(pl.multiple_of(16 * core, 16), 16), :]
         ycopies[f, dy] = go(
-            rcopy(src, wg.at[f, pl.ds(row, 16), :], sy.at[f, dy - 1], ry.at[f, dy - 1], place(x, y + dy, z, core))
+            rcopy(src, wg.at[f, :, pl.ds(row, 16), :], sy.at[f, dy - 1], ry.at[f, dy - 1], place(x, y + dy, z, core))
         )
 
     def x_send(f, dy):
         row = pl.multiple_of(shard_row(xl, lax.rem(y - dy + 4, 4)) + 16 * core, 16)
         for side in range(2):
+            lanes = pl.ds(side * 128, 128)
             if dy == 0:
-                src = filters[f].at[pl.ds(pl.multiple_of(16 * core, 16), 16), pl.ds(side * HALF, HALF)]
+                src = filters[f].at[:, pl.ds(pl.multiple_of(16 * core, 16), 16), lanes]
             else:
-                src = wg.at[f, pl.ds(row, 16), pl.ds(side * HALF, HALF)]
-            dst = wg.at[f, pl.ds(row, 16), pl.ds(side * HALF, HALF)]
+                src = wg.at[f, :, pl.ds(row, 16), lanes]
+            dst = wg.at[f, :, pl.ds(row, 16), lanes]
             xcopies[f, dy, side] = go(
                 rcopy(src, dst, sx.at[f, dy, side], rxs.at[f, dy, side], place(x + 1 - 2 * side, y, z, core))
             )
@@ -111,20 +119,22 @@
     def c_send(f, other, dy):
         xlo = 1 - xl if other else xl
         row = pl.multiple_of(shard_row(xlo, lax.rem(y - dy + 4, 4)) + 16 * core, 16)
-        ref = wg.at[f, pl.ds(row, 16), :]
+        ref = wg.at[f, :, pl.ds(row, 16), :]
         ccopies[f, other, dy] = go(rcopy(ref, ref, sc.at[f, other, dy], rcs.at[f, other, dy], partner))
 
-    def filter_start(f):
+    def own_shard(f):
+        wg[f, :, pl.ds(pl.multiple_of(shard_row(xl, y), 32), 32), :] = filters[f][...]
+
+    def filter_y(f):
         for dy in (1, 3, 2):
             y_send(f, dy)
-        x_send(f, 0)
-        wg[f, pl.ds(pl.multiple_of(shard_row(xl, y), 32), 32), :] = filters[f][...]
-
-    def filter_pass(f):
-        for dy in (1, 3, 2):
-            ycopies[f, dy].wait_recv()
-            x_send(f, dy)
-            c_send(f, 0, dy)
+
+    def filter_relay(f, dy):
+        ycopies[f, dy].wait_recv()
+        x_send(f, dy)
+        c_send(f, 0, dy)
+
+    def filter_swap(f):
         for dy in (0, 1, 3, 2):
             for side in range(2):
                 xcopies[f, dy, side].wait_recv()
@@ -150,7 +160,9 @@
     def joined(ref):
         return jnp.concatenate([ref[k] for k in range(ref.shape[0])], axis=1)
 
-    filter_start(0)
+    filter_y(0)
+    x_send(0, 0)
+    loads[1].wait()
 
     hcopies = []
     for v, (rows, dg) in enumerate(((RB - 4, 1), (0, NGY - 1))):
@@ -164,7 +176,11 @@
     hcopies.append(go(rcopy(colbuf.at[0], rc.at[0], sh.at[2, 0], rh.at[2, 0], at_gy(0, gxr))))
     hcopies.append(go(rcopy(colbuf.at[1], rc.at[1], sh.at[2, 1], rh.at[2, 1], at_gy(0, gxl))))
 
-    filter_start(1)
+    loads[2].wait()
+    filter_y(1)
+    own_shard(0)
+    own_shard(1)
+    loads[3].wait()
 
     split(out32, cot[...].astype(F32).reshape(32 * CB, 384))
     for c in range(CB):
@@ -172,13 +188,27 @@
     rows_k = lax.broadcasted_iota(jnp.int32, (768, 128), 0)
     lane = lax.broadcasted_iota(jnp.int32, (1, 128), 1)
     high = jnp.where(lane >= 64, 1, 0)
-    for b in range(NGY):
+
+    def cot_rows(b):
         row_of = 48 * b - 8 + lane - 64 * high
         target = jnp.where((row_of >= 0) & (row_of < 384), row_of + 384 * high, -1)
         sel1[...] = jnp.where(rows_k == target, 1.0, 0.0).astype(BF16)
         res = mm(bmat[...], sel1[...], NN).astype(BF16)
         for cp in range(8):
             sendc[b, :, pl.ds(cp * 128, 128)] = res[cp * 32:(cp + 1) * 32, :]
+
+    filter_relay(0, 1)
+    filter_relay(0, 3)
+    for b in range(4):
+        cot_rows(b)
+    filter_relay(0, 2)
+    for b in range(4, NGY):
+        cot_rows(b)
+    filter_swap(0)
+    x_send(1, 0)
+    for dy in (1, 3, 2):
+        filter_relay(1, dy)
+
     row = pl.multiple_of(gy * 32, 32)
     cotcopies = []
     for d in range(1, NGY):
@@ -193,8 +223,6 @@
             dst = cott.at[pl.ds(row, 32), pl.ds(0 if side == 1 else 1152, 128)]
             cotcopies.append(go(rcopy(src, dst, scot.at[side, d], rcot.at[side, d], dev)))
     cott[pl.ds(row, 32), pl.ds(128, 1024)] = sendc[gy]
-
-    filter_pass(0)
 
     p32[...] = jnp.zeros_like(p32)
     for c in range(CB):
@@ -224,7 +252,7 @@
     filter_end(0)
 
     def tap(f, i, j):
-        return wg[f, :, pl.ds((i * 3 + j) * CH, CH)]
+        return wg[f, i * 3 + j]
 
     def taps_in(f, j):
         return jnp.concatenate([tap(f, i, j) for i in range(3)], axis=1)
@@ -239,7 +267,7 @@
             acc = term if acc is None else acc + term
         pre1[pl.ds(t * 704, 704), :] = acc
 
-    filter_pass(1)
+    filter_swap(1)
 
     row_in = lax.broadcasted_iota(jnp.int32, (ST, CH), 0) + (48 * gy - 8)
     rows_ok = (row_in >= 0) & (row_in < 384)
@@ -282,32 +310,31 @@
         outs[:, :, pl.ds(t * 256 + lo - 128, hi - lo)] = act[:, :, lo:hi]
         otb[:, pl.ds(t * 256 + lo - 128, hi - lo)] = own[:, lo:hi]
 
-    outcopies = []
-    for d in range(1, NGY):
-        dev = at_gy(d)
-        outcopies.append(go(rcopy(outs.at[dev["gy"]], rout.at[gy], so.at[d], ro.at[d], dev)))
-    rout[gy] = outs[gy]
-
     def grad(g, left, right, base):
+        copies = []
         for j in range(3):
             part = mm(left[...], right[pl.ds((base + j) * ST, 1024), :], NN)
             for i in range(3):
                 value = part[:, i * CH:(i + 1) * CH].reshape(8, 2, 16, CH)
-                gf[g, :, :, :, pl.ds((i * 3 + j) * CH, CH)] = value
-                gb[g, :, :, :, pl.ds((i * 3 + j) * CH, CH)] = value.astype(BF16)
-        return go(rcopy(gb.at[g, :, 1 - core], rb.at[g], sp.at[g], rp.at[g], partner))
+                gf[g, :, :, j * 3 + i] = value
+                gb[g, :, :, j * 3 + i] = value.astype(BF16)
+            taps = pl.ds(3 * j, 3)
+            copies.append(go(rcopy(gb.at[g, :, 1 - core, taps], rb.at[g, :, taps], sp.at[g, j], rp.at[g, j], partner)))
+        return copies
 
     def plane(g, pair):
-        pair.wait_recv()
+        for copy in pair:
+            copy.wait_recv()
 
         @pl.loop(0, NGY)
         def _(b):
             for k in range(2):
-                part = gf[g, b, core, :, pl.ds(k * HALF, HALF)] + rb[g, b, :, pl.ds(k * HALF, HALF)].astype(F32)
+                lanes = pl.ds(k * 128, 128)
+                part = gf[g, b, core, :, :, lanes] + rb[g, b, :, :, lanes].astype(F32)
                 sb[g, b, k] = part.astype(BF16)
 
         copies = []
-        for dx, dy in ((1, 0), (3, 0), (0, 1), (0, 3), (1, 1), (3, 3), (1, 3), (3, 1), (2, 0), (0, 2), (2, 1), (1, 2), (2, 3), (3, 2), (2, 2)):
+        for dx, dy in ((2, 2), (1, 2), (3, 2), (2, 1), (2, 3), (1, 1), (3, 3), (1, 3), (3, 1), (2, 0), (0, 2), (1, 0), (3, 0), (0, 1), (0, 3)):
             tx = lax.rem(x + dx, 4)
             dev = place(x + dx, y + dy, z, core)
             slot = dx * 4 + dy
@@ -315,6 +342,88 @@
                 go(rcopy(sb.at[g, dev["gy"], lax.div(tx, 2)], rx.at[g, slot], spl.at[g, slot], rpl.at[g, slot], dev))
             )
         return copies
+
+    def scatter_copy(g, owner, source):
+        return rcopy(tz.at[g, owner], rz.at[g, source], sz.at[g, owner], rzs.at[g, source], place(x, y, owner, core))
+
+    def tail_scatter(g, copies):
+        for copy in copies:
+            copy.wait_recv()
+        total = sb[g, gy, xh].astype(F32)
+        for slot in range(1, 16):
+            total = total + rx[g, slot].astype(F32)
+        total = total.astype(BF16)
+        for p in range(OWNERS):
+            for n in range(2):
+                tap = 2 * p + n
+                tz[g, p, n] = total[tap] if tap < 9 else jnp.zeros((16, 128), BF16)
+        for p in range(OWNERS):
+            @pl.when(z != p)
+            def _():
+                scatter_copy(g, p, z).start()
+
+    my_slot = z * 2 + xh
+
+    def gather_copies(g):
+        copies = []
+        for dz in (4, 3, 5, 2, 6, 1, 7, 0):
+            for dxh in (1, 0):
+                if dz or dxh:
+                    dev = place(x + 2 * dxh, y, z + dz, core)
+                    ref = fin.at[g, my_slot]
+                    copies.append(rcopy(ref, ref, sg.at[g, dz, dxh], rg.at[g, my_slot], dev))
+        return copies
+
+    def tail_gather(g):
+        @pl.when(z < OWNERS)
+        def _():
+            for source in range(8):
+                @pl.when(z != source)
+                def _():
+                    scatter_copy(g, z, source).wait_recv()
+            rz[g, z] = tz[g, z]
+            total = rz[g, 0].astype(F32)
+            for source in range(1, 8):
+                total = total + rz[g, source].astype(F32)
+            fin[g, my_slot] = total.astype(BF16)
+            for copy in gather_copies(g):
+                copy.start()
+
+    def tail_swap(g):
+        for q in range(2 * OWNERS):
+            @pl.when(my_slot != q)
+            def _():
+                ref = fin.at[g, q]
+                rcopy(ref, ref, sg.at[g, 0, 0], rg.at[g, q], partner).wait_recv()
+        return go(rcopy(fin.at[g], finp.at[g], sf.at[g], rf.at[g], partner))
+
+    grads_o = (g1_o, g2_o)
+
+    def tail_write(g, swap):
+        for ref, half in ((fin, core), (finp, 1 - core)):
+            if ref is finp:
+                swap.wait_recv()
+            rows = pl.ds(pl.multiple_of(16 * half, 16), 16)
+            for q in range(2 * OWNERS):
+                for n in range(2):
+                    tap = 2 * (q // 2) + n
+                    if tap < 9:
+                        place_of = (tap % 3) * 3 + tap // 3
+                        gv[g, place_of, rows, pl.ds((q % 2) * 128, 128)] = ref[g, q, n].astype(F32) * scale
+        store = pltpu.make_async_copy(gv.at[g], grads_o[g], sout.at[2 + g])
+        store.start()
+        return store
+
+    def tail_end(g):
+        for p in range(OWNERS):
+            @pl.when(z != p)
+            def _():
+                scatter_copy(g, p, z).wait_send()
+
+        @pl.when(z < OWNERS)
+        def _():
+            for copy in gather_copies(g):
+                copy.wait_send()
 
     pair2 = grad(1, otb, hs, 2)
 
@@ -348,13 +457,25 @@
 
     shifts(i32, is_, 18 * ST)
     plane1 = plane(0, pair1)
+    outcopies = []
+    for d in range(1, NGY):
+        dev = at_gy(d)
+        outcopies.append(go(rcopy(outs.at[dev["gy"]], rout.at[gy], so.at[d], ro.at[d], dev)))
+    rout[gy] = outs[gy]
+
     acc = None
     for j in range(3):
         term = mm(is_[pl.ds((2 - j) * ST, 1024), :], taps_out(0, j), NN)
         acc = term if acc is None else acc + term
     for c in range(CB):
         put_strided(ig32, c, RB, CB, acc[c * ST + 8:c * ST + 8 + RB, :])
-    ig_o[...] = joined(ig32).astype(BF16).reshape(RB, CB, CH)
+    igv[...] = joined(ig32).astype(BF16).reshape(RB, CB, CH)
+    stores = [pltpu.make_async_copy(igv, ig_o, sout.at[0])]
+    stores[0].start()
+
+    tail_scatter(1, plane2)
+    tail_gather(1)
+    tail_scatter(0, plane1)
 
     for copy in outcopies:
         copy.wait_recv()
@@ -372,51 +493,22 @@
         res = mm(amat[...], sel2[...], NN)
         for cp in range(8):
             put_strided(out32, 2 * cp + par, 32, CB, res[cp * 32:(cp + 1) * 32, :])
-    out_o[...] = joined(out32).astype(BF16).reshape(32, CB, 384)
-
-    for g, copies in ((1, plane2), (0, plane1)):
-        for copy in copies:
-            copy.wait_recv()
-        for k in range(3):
-            lanes = pl.ds(k * PIECE, PIECE)
-            total = sb[g, gy, xh, :, lanes].astype(F32)
-            for slot in range(1, 16):
-                total = total + rx[g, slot, :, lanes].astype(F32)
-            tz[g * 3 + k] = total.astype(BF16)
-    tz[pl.ds(6, 2)] = jnp.zeros((2, 16, PIECE), BF16)
-    zcopies = []
-    for dz in (1, 7, 2, 6, 3, 5, 4):
-        zt = lax.rem(z + dz, 8)
-        zcopies.append(go(rcopy(tz.at[zt], rz.at[dz], sz.at[dz], rzs.at[dz], place(x, y, z + dz, core))))
-    for copy in zcopies:
-        copy.wait_recv()
-    total = tz[z].astype(F32)
-    for dz in range(1, 8):
-        total = total + rz[dz].astype(F32)
-    slot = z * 2 + xh
-    fin[slot] = total.astype(BF16)
-    gcopies = []
-    for dz in range(8):
-        for dxh in range(2):
-            if dz or dxh:
-                gcopies.append(
-                    go(rcopy(fin.at[slot], fin.at[slot], sg.at[dz, dxh], rg.at[dz, dxh], place(x + 2 * dxh, y, z + dz, core)))
-                )
-    for copy in gcopies:
-        copy.wait_recv()
-    last = go(rcopy(fin.at[pl.ds(0, 12)], finp, sf, rf, partner))
-    mine = pl.multiple_of(16 * core, 16)
-    theirs = pl.multiple_of(16 - 16 * core, 16)
-    outs_g = (g1_o, g2_o)
-    for q in range(12):
-        lanes = pl.ds((q % 2) * HALF + ((q // 2) % 3) * PIECE, PIECE)
-        outs_g[q // 6][pl.ds(mine, 16), lanes] = fin[q].astype(F32) * scale
-    last.wait_recv()
-    for q in range(12):
-        lanes = pl.ds((q % 2) * HALF + ((q // 2) % 3) * PIECE, PIECE)
-        outs_g[q // 6][pl.ds(theirs, 16), lanes] = finp[q].astype(F32) * scale
+    outv[...] = joined(out32).astype(BF16).reshape(32, CB, 384)
+    stores.append(pltpu.make_async_copy(outv, out_o, sout.at[1]))
+    stores[1].start()
+
+    tail_gather(0)
+    swap2 = tail_swap(1)
+    stores.append(tail_write(1, swap2))
+    swap1 = tail_swap(0)
+    stores.append(tail_write(0, swap1))
+
     for copy in pending:
         copy.wait_send()
+    tail_end(1)
+    tail_end(0)
+    for store in stores:
+        store.wait()
 
 
 def solution(mesh):
@@ -424,6 +516,13 @@
     vm = pltpu.VMEM
     dma = pltpu.SemaphoreType.DMA
     scratch = [
+        vm((RB, CB, CH), BF16),
+        vm((9, 32, CH), BF16),
+        vm((9, 32, CH), BF16),
+        vm((32, CB, 384), BF16),
+        vm((32, CB, 384), BF16),
+        vm((RB, CB, CH), BF16),
+        vm((2, 9, 32, CH), F32),
         vm((2, 768, 128), F32),
         vm((24 * ST + 16, CH), F32),
         vm((24 * ST, 768), BF16),
@@ -448,31 +547,32 @@
         vm((256, 1024), BF16),
         vm((1024, 384), BF16),
         vm((3, 512, 128), F32),
-        vm((2, CH, LANES), BF16),
+        vm((2, 9, CH, CH), BF16),
         vm((2, 4, RB, CH), BF16),
         vm((2, 4, RB, CH), BF16),
         vm((2, 3, 4, 16, CH), BF16),
         vm((2, 3, 2, 64, 128), F32),
-        vm((2, 8, 2, 16, LANES), F32),
-        vm((2, 8, 2, 16, LANES), BF16),
-        vm((2, 8, 16, LANES), BF16),
-        vm((2, 8, 2, 16, HALF), BF16),
-        vm((2, 16, 16, HALF), BF16),
-        vm((8, 16, PIECE), BF16),
-        vm((8, 16, PIECE), BF16),
-        vm((16, 16, PIECE), BF16),
-        vm((12, 16, PIECE), BF16),
+        vm((2, 8, 2, 9, 16, CH), F32),
+        vm((2, 8, 2, 9, 16, CH), BF16),
+        vm((2, 8, 9, 16, CH), BF16),
+        vm((2, 8, 2, 9, 16, 128), BF16),
+        vm((2, 16, 9, 16, 128), BF16),
+        vm((2, OWNERS, 2, 16, 128), BF16),
+        vm((2, 8, 2, 16, 128), BF16),
+        vm((2, 2 * OWNERS, 2, 16, 128), BF16),
+        vm((2, 2 * OWNERS, 2, 16, 128), BF16),
         dma((2, 3)), dma((2, 3)),
         dma((2, 4, 2)), dma((2, 4, 2)),
         dma((2, 2, 4)), dma((2, 2, 4)),
         dma((3, 3)), dma((3, 3)),
         dma((3, 8)), dma((3, 8)),
         dma((8,)), dma((8,)),
+        dma((2, 3)), dma((2, 3)),
+        dma((2, 16)), dma((2, 16)),
+        dma((2, OWNERS)), dma((2, 8)),
+        dma((2, 8, 2)), dma((2, 2 * OWNERS)),
         dma((2,)), dma((2,)),
-        dma((2, 16)), dma((2, 16)),
-        dma((8,)), dma((8,)),
-        dma((8, 2)), dma((8, 2)),
-        dma, dma,
+        dma((4,)), dma((4,)),
     ]
     call = pl.pallas_call(
         functools.partial(kernel, scale),
@@ -480,22 +580,26 @@
         out_shape=(
             jax.ShapeDtypeStruct((32, CB, 384), BF16),
             jax.ShapeDtypeStruct((RB, CB, CH), BF16),
-            jax.ShapeDtypeStruct((32, LANES), F32),
-            jax.ShapeDtypeStruct((32, LANES), F32),
+            jax.ShapeDtypeStruct((9, 32, CH), F32),
+            jax.ShapeDtypeStruct((9, 32, CH), F32),
         ),
-        in_specs=[pl.BlockSpec(memory_space=pltpu.VMEM)] * 4,
-        out_specs=[pl.BlockSpec(memory_space=pltpu.VMEM)] * 4,
+        in_specs=[pl.BlockSpec(memory_space=pl.ANY)] * 4,
+        out_specs=[pl.BlockSpec(memory_space=pl.ANY)] * 4,
         scratch_shapes=scratch,
         compiler_params=pltpu.CompilerParams(
             collective_id=0, has_side_effects=True, vmem_limit_bytes=60 * 1024 * 1024
         ),
     )
 
+    def taps_first(shard):
+        return jnp.transpose(shard, (1, 2, 0, 3)).reshape(9, 32, CH)
+
+    def taps_inside(grad):
+        return jnp.transpose(grad.reshape(3, 3, 32, CH), (2, 0, 1, 3))
+
     def body(features, first_filter, second_filter, cotangent):
-        out, ig, g1, g2 = call(
-            features, first_filter.reshape(32, LANES), second_filter.reshape(32, LANES), cotangent
-        )
-        return out, ig, g1.reshape(32, 3, 3, CH), g2.reshape(32, 3, 3, CH)
+        out, ig, g1, g2 = call(features, taps_first(first_filter), taps_first(second_filter), cotangent)
+        return out, ig, taps_inside(g1), taps_inside(g2)
 
     in_specs = (
         P("gy", "gx", None),

time: 89.8 us -> 81.3 us (0.905)
  Pallas kernels: 80.7 us -> 75.8 us
  local copies, waits for them, and re-layouts: 8.12 us -> 4.72 us
    pallas_call x1, Pallas kernels: 80.7 us -> 75.8 us  [body(): call(features, taps_first(first_filter), taps_first(second_filter), cotan...]
    reshape x4 -> x0, local copies, waits for them, and re-layouts: 2.92 us -> none  [the longest x2 1.27 us: body(): return (out, ig, g1.reshape(32, 3, 3, CH), g2.reshape(32, 3, 3, CH))]
    unnamed x14 -> x10, local copies, waits for them, and re-layouts: 5.19 us -> 4.72 us
where the time goes in v2:
time: 81.3 us; the launch traced here: 81.2 us
  Pallas kernels  75.8 us (93%)
  local copies, waits for them, and re-layouts  4.72 us (6%)
    pallas_call x1, Pallas kernels, body(): call(features, taps_first(first_filter), taps_first(second_filter), cotan...  75.8 us
    unnamed x10, local copies, waits for them, and re-layouts  4.72 us

profile of v2, /device:TPU:1, one launch (start us, length us, event | category | flops | bytes accessed | tf_op | source)
XLA Modules:
  0.0 81.2 jit_solution(13657190322126299138)
XLA Ops:
  0.6 75.8 %step.1 = (bf16[32,16,384]{2,1,0:T(8,128)(2,1)}, bf16[48,16,256]{2,1,0:T(8,128)(2,1)}, f32[9,32,256]{2,1,0:T(8,128)}, f32[9,32,256]{2,1,0:T(8,128)}) custom-call(bf16[48,16,256]{2,1,0:T(8,128)(2,1)} %feat_i.1, bf16[9,32,256]{2,1,0:T(8,128)(2,1)} %bitcast.14, bf16[9,32,256]{2,1,0:T(8,128)(2,1)} %bitcast.15, bf16[32,16,384]{2,1,0:T(8,128)(2,1)} %cot_i.1), custom_call_target="tpu_custom_call" | custom-call | tf_op jit(solution)/shard_map/step/pallas_call | solution.py:601
  76.4 0.0 copy-start
  76.4 1.8 %copy.12 = bf16[32,16,384]{2,1,0:T(8,128)(2,1)} copy(bf16[32,16,384]{2,1,0:T(8,128)(2,1)} %get-tuple-element.16) | data formatting | bytes 786432
  78.3 0.0 copy-done
  78.3 0.0 copy-start.2
  78.3 0.7 copy.13
  79.0 0.4 copy-done.2
  79.4 0.0 copy-start.1
  79.4 0.7 copy.14
  80.1 0.4 copy-done.1
  80.5 0.7 copy.15
Async XLA Ops:
  76.4 1.8 %copy-start = (bf16[48,16,256]{2,1,0:T(8,128)(2,1)S(1)}, bf16[48,16,256]{2,1,0:T(8,128)(2,1)}, u32[]{:S(2)}) copy-start(bf16[48,16,256]{2,1,0:T(8,128)(2,1)} %get-tuple-element.17) | copy-start | bytes 1179652
  78.3 1.1 %copy-start.2 = (f32[9,32,256]{2,1,0:T(8,128)S(1)}, f32[9,32,256]{2,1,0:T(8,128)}, u32[]{:S(2)}) copy-start(f32[9,32,256]{2,1,0:T(8,128)} %get-tuple-element.10) | copy-start | bytes 884740
  79.4 1.1 %copy-start.1 = (f32[9,32,256]{2,1,0:T(8,128)S(1)}, f32[9,32,256]{2,1,0:T(8,128)}, u32[]{:S(2)}) copy-start(f32[9,32,256]{2,1,0:T(8,128)} %get-tuple-element.11) | copy-start | bytes 884740
